TPU v7x, 128 devices: a whole 4x4x4 slice. The times are simulated.
128 devices in a mesh: row: 8 (over z, core), col: 16 (over y, x).
Axes of the slice: x: 4, y: 4, z: 4, core: 2. Of those that a mesh axis runs over, the one named last changes fastest.
Arguments:
- hidden: bfloat16 [1408, 16384], P('col', 'row'), may hold values from -18 to 18
- gain_in: bfloat16 [1408], replicated, may hold values from 0.5 to 1.5
- w_query: bfloat16 [1408, 1408], P('col'), may hold values from -0.3125 to 0.3125
- w_pair: bfloat16 [2, 1408, 1408], P(None, 'col'), may hold values from -0.15625 to 0.15625
- kv_cache: bfloat16 [2, 1408, 16384], P(None, 'col', 'row'), may hold values from -103 to 103
- recompute_rows: int32 [8, 200], P('row'), may hold values from 0 to 2047, as said below
- segment_ids: int32 [16384], P('row'), may hold values from -1 to 1, as said below
- w_out: bfloat16 [1408, 1408], P('col'), may hold values from -0.3125 to 0.3125
- gain_merge: bfloat16 [1408], replicated, may hold values from 0.5 to 1.5
- w_merge: bfloat16 [4, 1408, 1408], P(None, 'col'), may hold values from -0.078125 to 0.078125
- requests: int32 [8, 16, 85], P('row'), may hold values from -1 to 511, as said below
Outputs:
- delivered: bfloat16 [8, 16, 85, 1408], P('row', 'col')
Inputs may be any that keep to these rules, and one draw needn't show every extreme that they name: `segment_ids`: ids do not fall along the tokens except to -1 for the padding at the end; every image covers a multiple of 4 tokens and starts at a multiple of 4. `recompute_rows`: the 200 offsets of one index of row are distinct. `requests`: for each index of row, the lists of all owners together name each of its 512 merged tokens exactly once; unused slots hold -1 and follow the used ones.
All inputs are finite; a program needn't handle non-finite values.
Results may differ from a plain program's by a relative error of at most 0.025.
The roundings to bfloat16 on the way count: a program that leaves them out, or rounds other values in their place, can miss the bound.
Values may be sent and summed in bfloat16 or wider, within the bound.
A program may use at most 128 MiB of HBM per device.

v0:
```python
import jax
import jax.numpy as jnp
from jax import lax
from jax.sharding import PartitionSpec as P

HD = 88
EPSILON = 1e-06
MASKED = -1e30
KEY_BLOCK = 1024


def on_device(
    hidden,
    gain_in,
    w_query,
    w_pair,
    kv_cache,
    recompute_rows,
    segment_ids,
    w_out,
    gain_merge,
    w_merge,
    requests,
):
    local_width, tok_rows = hidden.shape
    model_width = w_query.shape[1]
    heads_here = local_width // HD
    score_scale = HD ** (-0.5)
    column_start = lax.axis_index("col") * local_width
    full_rows = lax.all_gather(hidden, "col", axis=0, tiled=True)
    full_float = full_rows.astype(jnp.float32)
    in_mean = jnp.sum(full_float, axis=0, keepdims=True) / model_width
    in_square = jnp.sum(full_float * full_float, axis=0, keepdims=True) / model_width
    normed = (
        (full_float - in_mean)
        * lax.rsqrt(in_square - in_mean * in_mean + EPSILON)
        * gain_in.astype(jnp.float32)[:, None]
    ).astype(jnp.bfloat16)
    queries = jnp.dot(w_query, normed, preferred_element_type=jnp.float32).astype(jnp.bfloat16)
    picked_rows = recompute_rows[0]
    normed_picked = jnp.take(normed, picked_rows, axis=1)
    fresh_pairs = jnp.dot(
        w_pair.reshape(2 * local_width, model_width),
        normed_picked,
        preferred_element_type=jnp.float32,
    )
    fresh_pairs = fresh_pairs.astype(jnp.bfloat16).reshape(2, local_width, -1)
    keys_values = kv_cache.at[:, :, picked_rows].set(fresh_pairs)
    query_heads = queries.reshape(heads_here, HD, tok_rows)
    segment_grid = segment_ids.reshape(1, 1, tok_rows)

    def take_block(carried, pair_block, segment_block):
        running_max, running_sum, weighted = carried
        key_block = pair_block[0].reshape(heads_here, HD, -1)
        value_block = pair_block[1].reshape(heads_here, HD, -1)
        scores = (
            jnp.einsum("hdq,hdk->hqk", query_heads, key_block, preferred_element_type=jnp.float32)
            * score_scale
        )
        allowed = (segment_ids[:, None] == segment_block[None, :])[None, :, :]
        new_max = jnp.maximum(running_max, jnp.max(jnp.where(allowed, scores, MASKED), axis=2))
        weights_exp = jnp.where(allowed, jnp.exp(scores - new_max[:, :, None]), 0.0)
        factor = jnp.exp(running_max - new_max)
        running_sum = running_sum * factor + jnp.sum(weights_exp, axis=2)
        product = jnp.einsum(
            "hqk,hdk->hdq",
            weights_exp.astype(jnp.bfloat16),
            value_block,
            preferred_element_type=jnp.float32,
        )
        weighted = weighted * factor[:, None, :] + product
        return (new_max, running_sum, weighted)

    starting = (
        jnp.full((heads_here, tok_rows), MASKED, jnp.float32),
        jnp.zeros((heads_here, tok_rows), jnp.float32),
        jnp.zeros((heads_here, HD, tok_rows), jnp.float32),
    )
    carried = starting
    pair_rows = lax.all_gather(keys_values, "row", axis=2, tiled=True)
    segment_rows = lax.all_gather(segment_grid, "row", axis=2, tiled=True)
    segment_line = segment_rows[0, 0]
    piece_rows = pair_rows.shape[2]
    whole_blocks = piece_rows // KEY_BLOCK

    def loop_body(block_index, loop_state):
        pair_block = lax.dynamic_slice_in_dim(pair_rows, block_index * KEY_BLOCK, KEY_BLOCK, 2)
        segment_block = lax.dynamic_slice_in_dim(
            segment_line, block_index * KEY_BLOCK, KEY_BLOCK, 0
        )
        return take_block(loop_state, pair_block, segment_block)

    carried = lax.fori_loop(0, whole_blocks, loop_body, carried)
    running_max, running_sum, weighted = carried
    attended = (
        (weighted / running_sum[:, None, :]).astype(jnp.bfloat16).reshape(local_width, tok_rows)
    )
    gain_part = lax.dynamic_slice_in_dim(gain_merge, column_start, local_width, 0).astype(
        jnp.float32
    )[:, None]
    partial_out = lax.dot_general(
        w_out, attended, (((0,), (0,)), ((), ())), preferred_element_type=jnp.float32
    )
    summed = lax.psum(partial_out.astype(jnp.bfloat16), "col").astype(jnp.float32)
    updated = full_float + summed
    row_mean = jnp.sum(updated, axis=0, keepdims=True) / model_width
    row_square = jnp.sum(updated * updated, axis=0, keepdims=True) / model_width
    own_part = lax.dynamic_slice_in_dim(updated, column_start, local_width, 0)
    merger_in = (
        (own_part - row_mean) * lax.rsqrt(row_square - row_mean * row_mean + EPSILON) * gain_part
    ).astype(jnp.bfloat16)
    merged_rows = tok_rows // 4
    grouped = merger_in.reshape(local_width, merged_rows, 4)
    merged = jnp.einsum("cgi,icd->gd", grouped, w_merge, preferred_element_type=jnp.float32)
    wanted_rows = requests[0]
    is_valid = wanted_rows >= 0
    safe_index = jnp.where(is_valid, wanted_rows, 0)
    picked = jnp.where(is_valid[:, :, None], merged[safe_index], 0.0)
    owned_rows = lax.psum_scatter(
        picked.astype(jnp.bfloat16), "col", scatter_dimension=0, tiled=True
    )
    return owned_rows.reshape(1, 1, owned_rows.shape[1], model_width)


def solution(mesh):
    placed = (
        P("col", "row"),
        P(),
        P("col", None),
        P(None, "col", None),
        P(None, "col", "row"),
        P("row", None),
        P("row"),
        P("col", None),
        P(),
        P(None, "col", None),
        P("row", None, None),
    )
    return jax.shard_map(
        on_device,
        mesh=mesh,
        in_specs=placed,
        out_specs=P("row", "col", None, None),
        check_vma=False,
    )
```

profile of v0, /device:TPU:0, one launch (start us, length us, event | category | flops | bytes accessed | tf_op | source)
XLA Modules:
  0.0 632.6 jit_solution(8836994563244462151)
XLA Ops:
  11.8 59.0 %all-gather.4.cloned.1.call-done = bf16[1408,2048]{1,0:T(8,128)(2,1)} async-done(((bf16[88,2048]{1,0:T(8,128)(2,1)}), bf16[1408,2048]{1,0:T(8,128)(2,1)}) %all-gather.4.cloned.1.call-update) | async-done | bytes 5767184 | tf_op jit(solution)/shard_map/all_gather | solution.py:30
  70.7 8.4 %copy.22 = bf16[1408,2048]{0,1:T(8,128)(2,1)} copy(bf16[1408,2048]{1,0:T(8,128)(2,1)} %all-gather.4.cloned.1.call-done) | data formatting | bytes 11534336 | tf_op jit(solution)/shard_map/all_gather | solution.py:30
  93.2 6.9 %scatter_fusion = bf16[2,88,2048]{1,0,2:T(2,128)(2,1)S(1)} fusion(bf16[2,88,2048]{1,0,2:T(2,128)(2,1)S(1)} %copy.24, s32[200]{0:T(256)S(1)} %bitcast.104, bf16[200,2,88]{2,1,0:T(2,128)(2,1)S(1)} %bitcast.99), kind=kCustom, calls=%fused_computation.2 | custom fusion | bytes 212000 | tf_op jit(solution)/shard_map/scatter | solution.py:48
  102.1 13.4 %all-gather = s32[16384]{0:T(1024)S(1)} all-gather(s32[2048]{0:T(1024)S(1)} %copy-done.2), channel_id=2, replica_groups=mesh['row'=8,'col'=16] {'row'}, dimensions={0}, use_global_device_ids=true | all-gather | bytes 73728 | tf_op jit(solution)/shard_map/all_gather | solution.py:81
  120.2 20.6 %all-gather.6.cloned.1.call-done = bf16[2,88,16384]{2,1,0:T(8,128)(2,1)} async-done(((bf16[2,88,2048]{2,1,0:T(8,128)(2,1)}), bf16[2,88,16384]{2,1,0:T(8,128)(2,1)}) %all-gather.6.cloned.1.call-update) | async-done | bytes 5767184 | tf_op jit(solution)/shard_map/all_gather | solution.py:80
  140.9 249.8 %while.18 = (s32[]{:T(128)}, f32[1,2048]{1,0:T(1,128)S(1)}, f32[1,2048]{1,0:T(1,128)S(1)}, f32[1,88,2048]{2,1,0:T(8,128)S(1)}, s32[2048]{0:T(1024)S(1)}, /*index...) while((s32[]{:T(128)}, f32[1,2048]{1,0:T(1,128)S(1)}, ...), condition=%wide.region_6.7_spmd.clone, body=%wide.region_3.0_spmd.clone.sunk | while | flops 768108544 | bytes 27504848 | solution.py:93
  140.9 5.6 fusion.46
  156.5 5.5 fusion.46
  172.1 5.5 fusion.46
  187.7 5.5 fusion.46
  203.4 5.5 fusion.46
  219.0 5.5 fusion.46
  234.6 5.5 fusion.46
  250.2 5.5 fusion.46
  265.8 5.5 fusion.46
  281.4 5.5 fusion.46
  312.6 5.5 fusion.46
  343.9 5.5 fusion.46
  359.5 5.5 fusion.46
  375.1 5.5 fusion.46
  396.1 116.2 %all-reduce.3.cloned.1.call-done = bf16[1408,2048]{0,1:T(8,128)(2,1)} async-done(((bf16[1408,2048]{0,1:T(8,128)(2,1)}), bf16[1408,2048]{0,1:T(8,128)(2,1)}) %all-reduce.3.cloned.1.call-update) | async-done | bytes 5767184 | tf_op jit(solution)/shard_map/psum | solution.py:104
  512.3 10.2 %fusion.33 = (f32[2048]{0:T(1024)S(1)}, f32[2048]{0:T(1024)S(1)}, f32[1408,2048]{0,1:T(8,128)}) fusion(bf16[1408,2048]{0,1:T(8,128)(2,1)} %all-reduce.3.cloned.1.call-done, bf16[1408,2048]{0,1:T(8,128)(2,1)} %copy.22), kind=kLoop, calls=%fused_computation.65 | loop fusion | flops 17297408 | bytes 23085056 | tf_op jit(solution)/shard_map/reduce_sum | solution.py:106
  526.0 6.0 gather_fusion.1
  539.8 86.3 %reduce-scatter.4.cloned.1.call-done = bf16[1,85,1408]{2,1,0:T(8,128)(2,1)} async-done(((bf16[16,85,1408]{2,1,0:T(8,128)(2,1)}), bf16[1,85,1408]{2,1,0:T(8,128)(2,1)}) %reduce-scatter.4.cloned.1.call-update) | async-done | bytes 239376
  (147 shorter events, 214.2 us)
Async XLA Ops:
  6.5 518.4 %copy-start = (bf16[4,88,1408]{2,1,0:T(8,128)(2,1)S(1)}, bf16[4,88,1408]{2,1,0:T(8,128)(2,1)}, u32[]{:S(2)}) copy-start(bf16[4,88,1408]{2,1,0:T(8,128)(2,1)} %param.22) | copy-start | bytes 2973700
  6.5 64.2 %all-gather.4.cloned.1.call-start = ((), (), s32[]{:S(2)}) async-start(), calls=%async_computation.1 | async-start | bytes 6127616 | tf_op jit(solution)/shard_map/all_gather | solution.py:30
  7.3 133.6 %all-gather.6.cloned.1.call-start = ((), (), s32[]{:S(2)}) async-start(), calls=%async_computation.2 | async-start | bytes 6488064 | tf_op jit(solution)/shard_map/all_gather | solution.py:80
  79.1 4.5 copy-start.1
  83.6 9.0 %copy-start.6 = (bf16[2,88,1408]{2,1,0:T(8,128)(2,1)S(1)}, bf16[2,88,1408]{2,1,0:T(8,128)(2,1)}, u32[]{:S(2)}) copy-start(bf16[2,88,1408]{2,1,0:T(8,128)(2,1)} %param.16) | copy-start | bytes 1486852
  87.6 14.5 %copy-start.2 = (s32[2048]{0:T(1024)S(1)}, s32[2048]{0:T(1024)}, u32[]{:S(2)}) copy-start(s32[2048]{0:T(1024)} %param.19) | copy-start | bytes 24580
  87.6 27.9 %copy-start.3 = (bf16[88,1408]{1,0:T(8,128)(2,1)S(1)}, bf16[88,1408]{1,0:T(8,128)(2,1)}, u32[]{:S(2)}) copy-start(bf16[88,1408]{1,0:T(8,128)(2,1)} %param.15) | copy-start | bytes 743428
  102.1 410.2 %all-reduce.3.cloned.1.call-start = ((), (), s32[]{:S(2)}) async-start(), calls=%async_computation.3 | async-start | bytes 11534336 | tf_op jit(solution)/shard_map/psum | solution.py:104
  140.9 249.8 %copy-start.4 = (bf16[88,1408]{1,0:T(8,128)(2,1)S(1)}, bf16[88,1408]{1,0:T(8,128)(2,1)}, u32[]{:S(2)}) copy-start(bf16[88,1408]{1,0:T(8,128)(2,1)} %param.20) | copy-start | bytes 743428
  390.7 4.5 copy-start.5
  395.0 231.1 %reduce-scatter.4.cloned.1.call-start = ((), (), s32[]{:S(2)}) async-start(), calls=%async_computation.4 | async-start | bytes 4212736
Sparse Core Ops, SparseCore 0:
  9.5 61.1 all-gather.3
  102.2 38.6 all-gather.5
  395.1 117.1 all-reduce.2
  539.9 86.1 reduce-scatter.3
where the time goes:
time: 634 us; the launch traced here: 633 us
  waiting for transfers between devices  283 us (45%)
  matrix products  185 us (29%)
  other arithmetic  102 us (16%)
  local copies, waits for them, and re-layouts  35 us (6%)
  blocking collectives  13.4 us (2%)
  between operations  13.3 us (2%)
    psum x1, waiting for transfers between devices, on_device(): lax.psum(partial_out.astype(jnp.bfloat16), 'col').astype(jnp.float32)  116 us
    dot_general x16, matrix products, take_block(): jnp.einsum('hdq,hdk->hqk', query_heads, key_block, preferred_element_type...  88.5 us
    unnamed x5, waiting for transfers between devices  87 us
    dot_general x16, matrix products, take_block(): jnp.einsum('hqk,hdk->hdq', weights_exp.astype(jnp.bfloat16), value_block,...  86.2 us
    reduce_sum x16, other arithmetic, take_block(): running_sum = running_sum * factor + jnp.sum(weights_exp, axis=2)  73.2 us
    all_gather x1, waiting for transfers between devices, on_device(): full_rows = lax.all_gather(hidden, 'col', axis=0, tiled=True)  59 us
    all_gather x1, waiting for transfers between devices, on_device(): pair_rows = lax.all_gather(keys_values, 'row', axis=2, tiled=True)  20.6 us
    all_gather x1, blocking collectives, on_device(): segment_rows = lax.all_gather(segment_grid, 'row', axis=2, tiled=True)  13.4 us
  transfers between devices with their start and end apart: 4, of which 4 were waited for; matrix products, arithmetic and copies ran while one was open for 2% of the time, Pallas kernels for 0%

commit v1 on v0

--- a/solution.py
+++ b/solution.py
@@ -77,7 +77,8 @@
         jnp.zeros((heads_here, HD, tok_rows), jnp.float32),
     )
     carried = starting
-    pair_rows = lax.all_gather(keys_values, "row", axis=2, tiled=True)
+    sent = jnp.stack([keys_values] * lax.axis_size("row"))
+    pair_rows = jnp.concatenate(lax.all_to_all(sent, "row", 0, 0), axis=2)
     segment_rows = lax.all_gather(segment_grid, "row", axis=2, tiled=True)
     segment_line = segment_rows[0, 0]
     piece_rows = pair_rows.shape[2]

time: 634 us -> 684 us (1.079)
  blocking collectives: 13.4 us -> 72.2 us
  waiting for transfers between devices: 283 us -> 261 us
  local copies, waits for them, and re-layouts: 35 us -> 43 us
    all_gather x1, blocking collectives: 13.4 us -> 72.2 us  [on_device(): segment_rows = lax.all_gather(segment_grid, 'row', axis=2, tiled=True)]
    all_gather x1 -> x0, waiting for transfers between devices: 20.6 us -> none  [on_device(): pair_rows = lax.all_gather(keys_values, 'row', axis=2, tiled=True)]
    unnamed x5 -> x4, waiting for transfers between devices: 87 us -> 87 us
  transfers between devices with their start and end apart: 4 -> 4, of which waited for: 4 -> 3; matrix products, arithmetic and copies ran while one was open for 2% -> 1% of each run, Pallas kernels for 0% -> 0%
where the time goes in v1:
time: 684 us; the launch traced here: 683 us
  waiting for transfers between devices  261 us (38%)
  matrix products  185 us (27%)
  other arithmetic  102 us (15%)
  blocking collectives  72.2 us (11%)
  local copies, waits for them, and re-layouts  43 us (6%)
  between operations  13.3 us (2%)
    psum x1, waiting for transfers between devices, on_device(): lax.psum(partial_out.astype(jnp.bfloat16), 'col').astype(jnp.float32)  115 us
    dot_general x16, matrix products, take_block(): jnp.einsum('hdq,hdk->hqk', query_heads, key_block, preferred_element_type...  88.6 us
    unnamed x4, waiting for transfers between devices  87 us
    dot_general x16, matrix products, take_block(): jnp.einsum('hqk,hdk->hdq', weights_exp.astype(jnp.bfloat16), value_block,...  86.4 us
    reduce_sum x16, other arithmetic, take_block(): running_sum = running_sum * factor + jnp.sum(weights_exp, axis=2)  73.2 us
    all_gather x1, blocking collectives, on_device(): segment_rows = lax.all_gather(segment_grid, 'row', axis=2, tiled=True)  72.2 us
    all_gather x1, waiting for transfers between devices, on_device(): full_rows = lax.all_gather(hidden, 'col', axis=0, tiled=True)  59 us
  transfers between devices with their start and end apart: 4, of which 3 were waited for; matrix products, arithmetic and copies ran while one was open for 1% of the time, Pallas kernels for 0%

profile of v1, /device:TPU:0, one launch (start us, length us, event | category | flops | bytes accessed | tf_op | source)
XLA Modules:
  0.0 682.6 jit_solution(6239626202895411671)
XLA Ops:
  11.7 59.0 %all-gather.3.cloned.1.call-done = bf16[1408,2048]{1,0:T(8,128)(2,1)} async-done(((bf16[88,2048]{1,0:T(8,128)(2,1)}), bf16[1408,2048]{1,0:T(8,128)(2,1)}) %all-gather.3.cloned.1.call-update) | async-done | bytes 5767184 | tf_op jit(solution)/shard_map/all_gather | solution.py:30
  70.7 8.4 %copy.27 = bf16[1408,2048]{0,1:T(8,128)(2,1)} copy(bf16[1408,2048]{1,0:T(8,128)(2,1)} %all-gather.3.cloned.1.call-done) | data formatting | bytes 11534336 | tf_op jit(solution)/shard_map/all_gather | solution.py:30
  93.1 6.9 %scatter_fusion = bf16[2,88,2048]{1,0,2:T(2,128)(2,1)S(1)} fusion(bf16[2,88,2048]{1,0,2:T(2,128)(2,1)S(1)} %copy.29, s32[200]{0:T(256)S(1)} %bitcast.108, bf16[200,2,88]{2,1,0:T(2,128)(2,1)S(1)} %bitcast.103), kind=kCustom, calls=%fused_computation.2 | custom fusion | bytes 212000 | tf_op jit(solution)/shard_map/scatter | solution.py:48
  108.8 72.2 %all-gather = s32[16384]{0:T(1024)S(1)} all-gather(s32[2048]{0:T(1024)S(1)} %copy-done.2), channel_id=2, replica_groups=mesh['row'=8,'col'=16] {'row'}, dimensions={0}, use_global_device_ids=true | all-gather | bytes 73728 | tf_op jit(solution)/shard_map/all_gather | solution.py:82
  185.7 6.1 copy.33
  191.8 250.1 %while.18 = (s32[]{:T(128)}, f32[1,2048]{1,0:T(1,128)S(1)}, f32[1,2048]{1,0:T(1,128)S(1)}, f32[1,88,2048]{2,1,0:T(8,128)S(1)}, s32[2048]{0:T(1024)S(1)}, /*index...) while((s32[]{:T(128)}, f32[1,2048]{1,0:T(1,128)S(1)}, ...), condition=%wide.region_6.7_spmd.clone, body=%wide.region_3.0_spmd.clone.sunk | while | flops 768108544 | bytes 27504848 | solution.py:94
  191.8 5.6 fusion.46
  207.5 5.5 fusion.46
  223.1 5.5 fusion.46
  238.8 5.5 fusion.46
  254.4 5.5 fusion.46
  270.0 5.5 fusion.46
  285.7 5.5 fusion.46
  301.3 5.5 fusion.46
  316.9 5.5 fusion.46
  332.6 5.5 fusion.46
  363.8 5.5 fusion.46
  379.5 5.5 fusion.46
  395.1 5.5 fusion.46
  426.4 5.5 fusion.46
  447.4 114.9 %all-reduce.3.cloned.1.call-done = bf16[1408,2048]{0,1:T(8,128)(2,1)} async-done(((bf16[1408,2048]{0,1:T(8,128)(2,1)}), bf16[1408,2048]{0,1:T(8,128)(2,1)}) %all-reduce.3.cloned.1.call-update) | async-done | bytes 5767184 | tf_op jit(solution)/shard_map/psum | solution.py:105
  562.3 10.2 %fusion.33 = (f32[2048]{0:T(1024)S(1)}, f32[2048]{0:T(1024)S(1)}, f32[1408,2048]{0,1:T(8,128)}) fusion(bf16[1408,2048]{0,1:T(8,128)(2,1)} %all-reduce.3.cloned.1.call-done, bf16[1408,2048]{0,1:T(8,128)(2,1)} %copy.27), kind=kLoop, calls=%fused_computation.65 | loop fusion | flops 17297408 | bytes 23085056 | tf_op jit(solution)/shard_map/reduce_sum | solution.py:107
  576.0 6.0 gather_fusion.1
  589.8 86.2 %reduce-scatter.4.cloned.1.call-done = bf16[1,85,1408]{2,1,0:T(8,128)(2,1)} async-done(((bf16[16,85,1408]{2,1,0:T(8,128)(2,1)}), bf16[1,85,1408]{2,1,0:T(8,128)(2,1)}) %reduce-scatter.4.cloned.1.call-update) | async-done | bytes 239376
  (148 shorter events, 221.0 us)
Async XLA Ops:
  6.5 568.4 %copy-start = (bf16[4,88,1408]{2,1,0:T(8,128)(2,1)S(1)}, bf16[4,88,1408]{2,1,0:T(8,128)(2,1)}, u32[]{:S(2)}) copy-start(bf16[4,88,1408]{2,1,0:T(8,128)(2,1)} %param.22) | copy-start | bytes 2973700
  6.5 64.2 %all-gather.3.cloned.1.call-start = ((), (), s32[]{:S(2)}) async-start(), calls=%async_computation.2 | async-start | bytes 6127616 | tf_op jit(solution)/shard_map/all_gather | solution.py:30
  79.1 4.5 copy-start.1
  83.6 9.0 %copy-start.6 = (bf16[2,88,1408]{2,1,0:T(8,128)(2,1)S(1)}, bf16[2,88,1408]{2,1,0:T(8,128)(2,1)}, u32[]{:S(2)}) copy-start(bf16[2,88,1408]{2,1,0:T(8,128)(2,1)} %param.16) | copy-start | bytes 1486852
  100.8 8.0 %copy-start.2 = (s32[2048]{0:T(1024)S(1)}, s32[2048]{0:T(1024)}, u32[]{:S(2)}) copy-start(s32[2048]{0:T(1024)} %param.19) | copy-start | bytes 24580
  100.8 80.3 %copy-start.3 = (bf16[88,1408]{1,0:T(8,128)(2,1)S(1)}, bf16[88,1408]{1,0:T(8,128)(2,1)}, u32[]{:S(2)}) copy-start(bf16[88,1408]{1,0:T(8,128)(2,1)} %param.15) | copy-start | bytes 743428
  104.0 81.7 %all-to-all-start = ((bf16[8,2,88,2048]{3,2,1,0:T(8,128)(2,1)}), bf16[8,2,88,2048]{3,2,1,0:T(8,128)(2,1)}, u32[]{:S(2)}, u32[]{:S(2)}) async-start(bf16[8,2,88,2048]{3,2,1,0:T(8,128)(2,1)} %stack.2), calls=%async_computation | async-start | bytes 11534336 | tf_op jit(solution)/shard_map/all_to_all | solution.py:81
  108.7 453.6 %all-reduce.3.cloned.1.call-start = ((), (), s32[]{:S(2)}) async-start(), calls=%async_computation.3 | async-start | bytes 11534336 | tf_op jit(solution)/shard_map/psum | solution.py:105
  191.8 250.1 %copy-start.4 = (bf16[88,1408]{1,0:T(8,128)(2,1)S(1)}, bf16[88,1408]{1,0:T(8,128)(2,1)}, u32[]{:S(2)}) copy-start(bf16[88,1408]{1,0:T(8,128)(2,1)} %param.20) | copy-start | bytes 743428
  442.0 4.5 copy-start.5
  446.2 229.8 %reduce-scatter.4.cloned.1.call-start = ((), (), s32[]{:S(2)}) async-start(), calls=%async_computation.4 | async-start | bytes 4212736
Sparse Core Ops, SparseCore 0:
  9.5 61.1 all-gather.2
  446.3 115.9 all-reduce.2
  589.9 86.0 reduce-scatter.3
